TPU v7x, 32 devices: a whole 2x2x4 slice. The times are simulated.
32 devices in a mesh: grp: 2 (over x), seq: 16 (over z, y, core).
Axes of the slice: x: 2, y: 2, z: 4, core: 2. Of those that a mesh axis runs over, the one named last changes fastest.
Arguments:
- query_rows: bfloat16 [16384, 1536], P(('grp', 'seq')), parts along dimension 0, may hold values from -6 to 6
- key_rows: bfloat16 [16384, 1536], P(('grp', 'seq')), parts along dimension 0, may hold values from -6 to 6
- value_rows: bfloat16 [16384, 1536], P(('grp', 'seq')), parts along dimension 0, may hold values from -6 to 6
- doc_start: int32 [16384], P(('grp', 'seq')), parts along dimension 0, may hold values from 0 to 8191, as said below
Outputs:
- attention_out: bfloat16 [16384, 1536], P(('grp', 'seq')), parts along dimension 0
There are 2 independent parts, one for each index of `grp`. A program takes and returns all parts, laid end to end along the dimension named above; each array names one. Nothing has to cross between parts.
Inputs may be any that keep to these rules, and one draw needn't show every extreme that they name: `doc_start`: the position of the first token of the token's document: never falling, equal to the token's own position at a document's first token and constant up to the next one.
All inputs are finite; a program needn't handle non-finite values.
Results may differ from a plain program's by a relative error of at most 0.0038.
Values may be sent and summed in bfloat16 or wider, within the bound.
A program may use at most 64 MiB of HBM per device.

v0:
```python
import math

import jax
import jax.numpy as jnp
from jax import lax
from jax.sharding import PartitionSpec as P

AH = 12
DH = 128
WINDOW = 2048


def shifted(block, axis, distance):
    devices = range(lax.axis_size(axis))
    route = [(i - distance, i) for i in devices if i - distance in devices]
    return lax.ppermute(block, axis, route)


def local(query_rows, key_rows, value_rows, doc_start):
    shard_rows = query_rows.shape[0]
    halo_count = WINDOW // shard_rows
    shard_first = lax.axis_index("seq") * shard_rows
    stacked = jnp.stack([key_rows, value_rows])
    earlier_shards = [shifted(stacked, "seq", distance) for distance in range(halo_count, 0, -1)]
    gathered = jnp.concatenate(earlier_shards + [stacked], axis=1)
    query_place = shard_first + jnp.arange(shard_rows, dtype=jnp.int32)
    key_place = (
        shard_first
        - halo_count * shard_rows
        + jnp.arange((halo_count + 1) * shard_rows, dtype=jnp.int32)
    )
    allowed = (
        (key_place[None, :] <= query_place[:, None])
        & (key_place[None, :] > query_place[:, None] - WINDOW)
        & (key_place[None, :] >= doc_start[:, None])
    )
    scale = 1.0 / math.sqrt(DH)

    def one_head(head_index):
        column = head_index * DH
        query_one = lax.dynamic_slice_in_dim(query_rows, column, DH, 1)
        key_one = lax.dynamic_slice_in_dim(gathered[0], column, DH, 1)
        value_one = lax.dynamic_slice_in_dim(gathered[1], column, DH, 1)
        scores = (
            jnp.einsum("qd,kd->qk", query_one, key_one, preferred_element_type=jnp.float32) * scale
        )
        scores = jnp.where(allowed, scores, -jnp.inf)
        largest = jnp.max(scores, axis=1, keepdims=True)
        powers = jnp.exp(scores - largest)
        totals = jnp.sum(powers, axis=1, keepdims=True)
        mixed_head = (
            jnp.dot(powers.astype(jnp.bfloat16), value_one, preferred_element_type=jnp.float32)
            / totals
        )
        return mixed_head.astype(jnp.bfloat16)

    head_outputs = lax.map(one_head, jnp.arange(AH, dtype=jnp.int32))
    return head_outputs.transpose(1, 0, 2).reshape(shard_rows, AH * DH)


def solution(mesh):
    placed = (
        P(("grp", "seq"), None),
        P(("grp", "seq"), None),
        P(("grp", "seq"), None),
        P(("grp", "seq")),
    )
    return jax.shard_map(
        local, mesh=mesh, in_specs=placed, out_specs=P(("grp", "seq"), None), check_vma=False
    )
```

profile of v0, /device:TPU:24, one launch (start us, length us, event | category | flops | bytes accessed | tf_op | source)
XLA Modules:
  0.0 397.6 jit_solution(17272172224262933350)
XLA Ops:
  3.5 2.9 collective-permute-start.1
  10.3 64.9 %collective-permute-done = bf16[2,512,1536]{2,1,0:T(8,128)(2,1)} collective-permute-done((bf16[2,512,1536]{2,1,0:T(8,128)(2,1)S(1)}, bf16[2,512,1536]{2,1,0:T(8,128)(2,1)}, u32[]{:S(2)}, u32[]{:S(2)}) %collective-permute-start) | collective-permute-done | bytes 3145760 | tf_op jit(solution)/shard_map/ppermute | solution.py:16
  77.3 30.5 %collective-permute-done.1 = bf16[2,512,1536]{2,1,0:T(8,128)(2,1)} collective-permute-done((bf16[2,512,1536]{2,1,0:T(8,128)(2,1)S(1)}, bf16[2,512,1536]{2,1,0:T(8,128)(2,1)}, u32[]{:S(2)}, u32[]{:S(2)}) %collective-permute-start.1) | collective-permute-done | bytes 3145760 | tf_op jit(solution)/shard_map/ppermute | solution.py:16
  109.8 101.1 %collective-permute-done.2 = bf16[2,512,1536]{2,1,0:T(8,128)(2,1)} collective-permute-done((bf16[2,512,1536]{2,1,0:T(8,128)(2,1)S(1)}, bf16[2,512,1536]{2,1,0:T(8,128)(2,1)}, u32[]{:S(2)}, u32[]{:S(2)}) %collective-permute-start.2) | collective-permute-done | bytes 3145760 | tf_op jit(solution)/shard_map/ppermute | solution.py:16
  213.0 30.5 %collective-permute-done.3 = bf16[2,512,1536]{2,1,0:T(8,128)(2,1)} collective-permute-done((bf16[2,512,1536]{2,1,0:T(8,128)(2,1)S(1)}, bf16[2,512,1536]{2,1,0:T(8,128)(2,1)}, u32[]{:S(2)}, u32[]{:S(2)}) %collective-permute-start.3) | collective-permute-done | bytes 3145760 | tf_op jit(solution)/shard_map/ppermute | solution.py:16
  243.5 2.2 constant_dynamic-update-slice_fusion.2
  246.0 5.5 %copy-done = bf16[2,2560,1536]{2,1,0:T(8,128)(2,1)} copy-done((bf16[2,2560,1536]{2,1,0:T(8,128)(2,1)}, bf16[2,2560,1536]{2,1,0:T(8,128)(2,1)S(1)}, u32[]{:S(2)}) %copy-start) | copy-done | bytes 15728664
  251.5 144.6 %while.11 = (s32[]{:T(128)}, bf16[12,512,128]{1,2,0:T(8,128)(2,1)S(1)}, s32[12]{0:T(128)S(1)}, bf16[512,1536]{1,0:T(8,128)(2,1)}, bf16[2,2560,1536]{2,1,0:T(8,12...) while((s32[]{:T(128)}, ...), condition=%wide.region_3.4_spmd.clone, body=%wide.region_0.3_spmd.clone.sunk | while | flops 686947328 | bytes 49312956 | solution.py:57
  252.7 6.2 %fusion.33 = (bf16[1,2560,1536]{2,1,0:T(8,128)(2,1)S(1)}, bf16[1,2560,1536]{2,1,0:T(8,128)(2,1)S(1)}) fusion(bf16[2,2560,1536]{2,1,0:T(8,128)(2,1)} %get-tuple-element.179), kind=kLoop, calls=%fused_computation.27.clone.1 | loop fusion | bytes 31457280 | tf_op jit(solution)/shard_map/while/body/eval_jaxpr/slice | solution.py:43
  258.9 2.6 fusion.34
  264.7 6.2 %fusion.33 = (bf16[1,2560,1536]{2,1,0:T(8,128)(2,1)S(1)}, bf16[1,2560,1536]{2,1,0:T(8,128)(2,1)S(1)}) fusion(bf16[2,2560,1536]{2,1,0:T(8,128)(2,1)} %get-tuple-element.179), kind=kLoop, calls=%fused_computation.27.clone.1 | loop fusion | bytes 31457280 | tf_op jit(solution)/shard_map/while/body/eval_jaxpr/slice | solution.py:43
  271.0 2.6 fusion.34
  276.8 6.2 %fusion.33 = (bf16[1,2560,1536]{2,1,0:T(8,128)(2,1)S(1)}, bf16[1,2560,1536]{2,1,0:T(8,128)(2,1)S(1)}) fusion(bf16[2,2560,1536]{2,1,0:T(8,128)(2,1)} %get-tuple-element.179), kind=kLoop, calls=%fused_computation.27.clone.1 | loop fusion | bytes 31457280 | tf_op jit(solution)/shard_map/while/body/eval_jaxpr/slice | solution.py:43
  283.0 2.6 fusion.34
  288.9 6.2 %fusion.33 = (bf16[1,2560,1536]{2,1,0:T(8,128)(2,1)S(1)}, bf16[1,2560,1536]{2,1,0:T(8,128)(2,1)S(1)}) fusion(bf16[2,2560,1536]{2,1,0:T(8,128)(2,1)} %get-tuple-element.179), kind=kLoop, calls=%fused_computation.27.clone.1 | loop fusion | bytes 31457280 | tf_op jit(solution)/shard_map/while/body/eval_jaxpr/slice | solution.py:43
  295.1 2.6 fusion.34
  300.9 6.2 %fusion.33 = (bf16[1,2560,1536]{2,1,0:T(8,128)(2,1)S(1)}, bf16[1,2560,1536]{2,1,0:T(8,128)(2,1)S(1)}) fusion(bf16[2,2560,1536]{2,1,0:T(8,128)(2,1)} %get-tuple-element.179), kind=kLoop, calls=%fused_computation.27.clone.1 | loop fusion | bytes 31457280 | tf_op jit(solution)/shard_map/while/body/eval_jaxpr/slice | solution.py:43
  307.1 2.6 fusion.34
  312.9 6.2 %fusion.33 = (bf16[1,2560,1536]{2,1,0:T(8,128)(2,1)S(1)}, bf16[1,2560,1536]{2,1,0:T(8,128)(2,1)S(1)}) fusion(bf16[2,2560,1536]{2,1,0:T(8,128)(2,1)} %get-tuple-element.179), kind=kLoop, calls=%fused_computation.27.clone.1 | loop fusion | bytes 31457280 | tf_op jit(solution)/shard_map/while/body/eval_jaxpr/slice | solution.py:43
  319.2 2.6 fusion.34
  325.0 6.2 %fusion.33 = (bf16[1,2560,1536]{2,1,0:T(8,128)(2,1)S(1)}, bf16[1,2560,1536]{2,1,0:T(8,128)(2,1)S(1)}) fusion(bf16[2,2560,1536]{2,1,0:T(8,128)(2,1)} %get-tuple-element.179), kind=kLoop, calls=%fused_computation.27.clone.1 | loop fusion | bytes 31457280 | tf_op jit(solution)/shard_map/while/body/eval_jaxpr/slice | solution.py:43
  331.2 2.6 fusion.34
  337.0 6.2 %fusion.33 = (bf16[1,2560,1536]{2,1,0:T(8,128)(2,1)S(1)}, bf16[1,2560,1536]{2,1,0:T(8,128)(2,1)S(1)}) fusion(bf16[2,2560,1536]{2,1,0:T(8,128)(2,1)} %get-tuple-element.179), kind=kLoop, calls=%fused_computation.27.clone.1 | loop fusion | bytes 31457280 | tf_op jit(solution)/shard_map/while/body/eval_jaxpr/slice | solution.py:43
  343.3 2.6 fusion.34
  349.1 6.2 %fusion.33 = (bf16[1,2560,1536]{2,1,0:T(8,128)(2,1)S(1)}, bf16[1,2560,1536]{2,1,0:T(8,128)(2,1)S(1)}) fusion(bf16[2,2560,1536]{2,1,0:T(8,128)(2,1)} %get-tuple-element.179), kind=kLoop, calls=%fused_computation.27.clone.1 | loop fusion | bytes 31457280 | tf_op jit(solution)/shard_map/while/body/eval_jaxpr/slice | solution.py:43
  355.3 2.6 fusion.34
  361.1 6.2 %fusion.33 = (bf16[1,2560,1536]{2,1,0:T(8,128)(2,1)S(1)}, bf16[1,2560,1536]{2,1,0:T(8,128)(2,1)S(1)}) fusion(bf16[2,2560,1536]{2,1,0:T(8,128)(2,1)} %get-tuple-element.179), kind=kLoop, calls=%fused_computation.27.clone.1 | loop fusion | bytes 31457280 | tf_op jit(solution)/shard_map/while/body/eval_jaxpr/slice | solution.py:43
  367.4 2.6 fusion.34
  373.2 6.2 %fusion.33 = (bf16[1,2560,1536]{2,1,0:T(8,128)(2,1)S(1)}, bf16[1,2560,1536]{2,1,0:T(8,128)(2,1)S(1)}) fusion(bf16[2,2560,1536]{2,1,0:T(8,128)(2,1)} %get-tuple-element.179), kind=kLoop, calls=%fused_computation.27.clone.1 | loop fusion | bytes 31457280 | tf_op jit(solution)/shard_map/while/body/eval_jaxpr/slice | solution.py:43
  379.4 2.6 fusion.34
  385.2 6.2 %fusion.33 = (bf16[1,2560,1536]{2,1,0:T(8,128)(2,1)S(1)}, bf16[1,2560,1536]{2,1,0:T(8,128)(2,1)S(1)}) fusion(bf16[2,2560,1536]{2,1,0:T(8,128)(2,1)} %get-tuple-element.179), kind=kLoop, calls=%fused_computation.27.clone.1 | loop fusion | bytes 31457280 | tf_op jit(solution)/shard_map/while/body/eval_jaxpr/slice | solution.py:43
  391.5 2.6 fusion.34
  (82 shorter events, 45.4 us)
Async XLA Ops:
  2.2 73.0 %collective-permute-start = (bf16[2,512,1536]{2,1,0:T(8,128)(2,1)S(1)}, bf16[2,512,1536]{2,1,0:T(8,128)(2,1)}, u32[]{:S(2)}, u32[]{:S(2)}) collective-permute-start(bf16[2,512,1536]{2,1,0:T(8,128)(2,1)S(1)} %pad_maximum_fusion), channel_id=1, source_target_pairs={{0,4},{1,5},{2,6},{3,7},{4,8},{5,9},{6,10},{7,11},{8,12},{9,13},{1... | collective-permute-start | bytes 9437192 | tf_op jit(solution)/shard_map/ppermute | solution.py:16
  3.5 104.2 %collective-permute-start.1 = (bf16[2,512,1536]{2,1,0:T(8,128)(2,1)S(1)}, bf16[2,512,1536]{2,1,0:T(8,128)(2,1)}, u32[]{:S(2)}, u32[]{:S(2)}) collective-permute-start(bf16[2,512,1536]{2,1,0:T(8,128)(2,1)S(1)} %pad_maximum_fusion), channel_id=1, source_target_pairs={{0,3},{1,4},{2,5},{3,6},{4,7},{5,8},{6,9},{7,10},{8,11},{9,12},{10... | collective-permute-start | bytes 9437192 | tf_op jit(solution)/shard_map/ppermute | solution.py:16
  6.3 204.6 %collective-permute-start.2 = (bf16[2,512,1536]{2,1,0:T(8,128)(2,1)S(1)}, bf16[2,512,1536]{2,1,0:T(8,128)(2,1)}, u32[]{:S(2)}, u32[]{:S(2)}) collective-permute-start(bf16[2,512,1536]{2,1,0:T(8,128)(2,1)S(1)} %pad_maximum_fusion), channel_id=1, source_target_pairs={{0,2},{1,3},{2,4},{3,5},{4,6},{5,7},{6,8},{7,9},{8,10},{9,11},{10,... | collective-permute-start | bytes 9437192 | tf_op jit(solution)/shard_map/ppermute | solution.py:16
  8.3 235.2 %collective-permute-start.3 = (bf16[2,512,1536]{2,1,0:T(8,128)(2,1)S(1)}, bf16[2,512,1536]{2,1,0:T(8,128)(2,1)}, u32[]{:S(2)}, u32[]{:S(2)}) collective-permute-start(bf16[2,512,1536]{2,1,0:T(8,128)(2,1)S(1)} %pad_maximum_fusion), channel_id=1, source_target_pairs={{0,1},{1,2},{2,3},{3,4},{4,5},{5,6},{6,7},{7,8},{8,9},{9,10},{10,1... | collective-permute-start | bytes 9437192 | tf_op jit(solution)/shard_map/ppermute | solution.py:16
  109.8 135.9 %copy-start.1 = (bf16[512,1536]{1,0:T(8,128)(2,1)S(1)}, bf16[512,1536]{1,0:T(8,128)(2,1)}, u32[]{:S(2)}) copy-start(bf16[512,1536]{1,0:T(8,128)(2,1)} %param.8) | copy-start | bytes 4718596
  109.8 135.9 %copy-start.2 = (bf16[512,1536]{1,0:T(8,128)(2,1)S(1)}, bf16[512,1536]{1,0:T(8,128)(2,1)}, u32[]{:S(2)}) copy-start(bf16[512,1536]{1,0:T(8,128)(2,1)} %param.7) | copy-start | bytes 4718596
  213.0 38.4 %copy-start.4 = (s32[512]{0:T(512)S(1)}, s32[512]{0:T(512)}, u32[]{:S(2)}) copy-start(s32[512]{0:T(512)} %param.9) | copy-start | bytes 6148
  243.5 8.0 %copy-start.3 = (bf16[12,512,128]{1,2,0:T(8,128)(2,1)S(1)}, bf16[12,512,128]{1,2,0:T(8,128)(2,1)}, u32[]{:S(2)}) copy-start(bf16[12,512,128]{1,2,0:T(8,128)(2,1)} %custom-call.1) | copy-start | bytes 4718596
  245.9 5.5 %copy-start = (bf16[2,2560,1536]{2,1,0:T(8,128)(2,1)}, bf16[2,2560,1536]{2,1,0:T(8,128)(2,1)S(1)}, u32[]{:S(2)}) copy-start(bf16[2,2560,1536]{2,1,0:T(8,128)(2,1)S(1)} %constant_dynamic-update-slice_fusion.1) | copy-start | bytes 47185924
where the time goes:
time: 398 us
  waiting for transfers between devices  227 us (57%)
  local copies, waits for them, and re-layouts  98.7 us (25%)
  matrix products  42.8 us (11%)
  other arithmetic  12.6 us (3%)
  loops' own time  8.39 us (2%)
  starting transfers between devices  8 us (2%)
    ppermute x4, waiting for transfers between devices, shifted(): return lax.ppermute(block, axis, route)  227 us
    slice x12, local copies, waits for them, and re-layouts, one_head(): value_one = lax.dynamic_slice_in_dim(gathered[1], column, DH, 1)  74.5 us
    dot_general x12, matrix products, one_head(): jnp.einsum('qd,kd->qk', query_one, key_one, preferred_element_type=jnp.fl...  31.6 us
    unnamed x14, local copies, waits for them, and re-layouts  14 us
    dot_general x12, matrix products, one_head(): jnp.dot(powers.astype(jnp.bfloat16), value_one, preferred_element_type=jn...  11.2 us
    reduce_sum x12, other arithmetic, one_head(): totals = jnp.sum(powers, axis=1, keepdims=True)  10.2 us
    another operation x1, loops' own time, local(): head_outputs = lax.map(one_head, jnp.arange(AH, dtype=jnp.int32))  8.39 us
    ppermute x4, starting transfers between devices, shifted(): return lax.ppermute(block, axis, route)  8 us
  transfers between devices with their start and end apart: 4, of which 4 were waited for; matrix products, arithmetic and copies ran while one was open for 2% of the time, Pallas kernels for 0%

commit v1 on v0

v1 whole, which is shorter than its diff:
```python
import functools
import math

import jax
import jax.numpy as jnp
from jax import lax
from jax.experimental import pallas as pl
from jax.experimental.pallas import tpu as pltpu
from jax.sharding import PartitionSpec as P

AH = 12
DH = 128
WINDOW = 2048
SPAN = 768
MESH = pl.DeviceIdType.MESH
HIDDEN = -1e30


def kernel(n, rows, ahead, doc_ref, q_hbm, k_hbm, v_hbm, out_ref,
           q_buf, k_buf, v_buf, low, own_sem, send_sem, recv_sem):
    group = lax.axis_index("grp")
    me = lax.axis_index("seq")
    upper = (me // 2) % 2
    odd = me % 2
    beside = me + 2 - 4 * upper
    twin = me + 1 - 2 * odd
    half = rows // 2
    sources = (k_hbm, v_hbm)
    buffers = (k_buf, v_buf)

    def columns(ref, head):
        return ref.at[:, pl.ds(pl.multiple_of(head * DH, DH), DH)]

    def slot(which, head, shard):
        return buffers[which].at[head, pl.ds(shard * rows, rows), :]

    def own_copies(head):
        pairs = [(q_hbm, q_buf.at[head])] + [(sources[w], slot(w, head, 4)) for w in (0, 1)]
        return [
            pltpu.make_async_copy(columns(source, head), target, own_sem.at[at, head])
            for at, (source, target) in enumerate(pairs)
        ]

    landing = (0, 2, 3, 1)

    def copies(kind, head, source_shard, target):
        made = []
        for w in (0, 1):
            source = columns(sources[w], head) if source_shard is None else slot(w, head, source_shard)
            made.append(pltpu.make_async_remote_copy(
                src_ref=source,
                dst_ref=slot(w, head, landing[kind]),
                send_sem=send_sem.at[kind, w, head],
                recv_sem=recv_sem.at[kind, w, head],
                device_id=(group, target),
                device_id_type=MESH,
            ))
        return made

    def begin(condition, kind, head, source_shard, target):
        @pl.when(condition)
        def _():
            for copy in copies(kind, head, source_shard, target):
                copy.start()

    def arrived(kind, head, condition):
        @pl.when(condition)
        def _():
            for copy in copies(kind, head, None, twin):
                copy.wait_recv()

    def send_own(head):
        begin(me + 4 < n, 0, head, None, me + 4)
        begin(upper == 0, 1, head, None, beside)
        begin(odd == 0, 2, head, None, twin)

    def sent(head):
        for kind, condition in (
            (0, me + 4 < n),
            (1, (upper == 0) | (me >= 4)),
            (2, (odd == 0) | (me >= 2)),
            (3, ((odd == 0) & (me >= 2)) | (me >= 5)),
        ):
            @pl.when(condition)
            def _():
                for copy in copies(kind, head, None, twin):
                    copy.wait_send()

    barrier = pltpu.get_barrier_semaphore()
    pl.semaphore_signal(barrier, inc=1, device_id=(group, beside), device_id_type=MESH)
    pl.semaphore_signal(barrier, inc=1, device_id=(group, twin), device_id_type=MESH)

    @pl.when(me >= 4)
    def _():
        pl.semaphore_signal(barrier, inc=1, device_id=(group, me - 4), device_id_type=MESH)

    @pl.when(me + 4 < n)
    def _():
        pl.semaphore_signal(barrier, inc=1, device_id=(group, me + 4), device_id_type=MESH)

    peers = 2 + (me >= 4).astype(jnp.int32) + (me + 4 < n).astype(jnp.int32)
    pl.semaphore_wait(barrier, peers)

    def first(head, carry):
        send_own(head)
        return carry

    lax.fori_loop(0, ahead, first, 0)

    def fetch(head, carry):
        for copy in own_copies(head):
            copy.start()
        return carry

    lax.fori_loop(0, AH, fetch, 0)

    for shard in range(4):
        @pl.when(me < 4 - shard)
        def _():
            def clear(head, carry):
                for buffer in buffers:
                    buffer[head, pl.ds(shard * rows, rows), :] = jnp.zeros((rows, DH), jnp.bfloat16)
                return carry

            lax.fori_loop(0, AH, clear, 0)

    row = lax.broadcasted_iota(jnp.int32, (rows, DH), 0)
    low[...] = jnp.maximum(doc_ref[...] - (me * rows - WINDOW), row + 1)

    scale = math.log2(math.e) / math.sqrt(DH)

    def attend(head):
        for part in range(2):
            span = slice(part * half, (part + 1) * half)
            queries = q_buf[head, span, :]
            lowest = low[span, 0:1]
            largest = jnp.full((half, 1), HIDDEN, jnp.float32)
            total = jnp.zeros((half, 1), jnp.float32)
            mixed = jnp.zeros((half, DH), jnp.float32)
            count = (WINDOW + half) // SPAN
            for step in range(count):
                start = part * half + step * SPAN
                keys = k_buf[head, start:start + SPAN, :]
                values = v_buf[head, start:start + SPAN, :]
                scores = lax.dot_general(
                    queries, keys, (((1,), (1,)), ((), ())), preferred_element_type=jnp.float32
                )
                place = start + lax.broadcasted_iota(jnp.int32, (half, SPAN), 1)
                allowed = place >= lowest
                if step == count - 1:
                    query = part * half + lax.broadcasted_iota(jnp.int32, (half, SPAN), 0)
                    allowed = allowed & (place <= query + WINDOW)
                scores = jnp.where(allowed, scores, HIDDEN)
                higher = jnp.maximum(largest, jnp.max(scores, axis=1, keepdims=True))
                powers = jnp.exp2((scores - higher) * scale)
                fade = jnp.exp2((largest - higher) * scale)
                total = total * fade + jnp.sum(powers, axis=1, keepdims=True)
                mixed = mixed * fade + jnp.dot(
                    powers.astype(jnp.bfloat16), values, preferred_element_type=jnp.float32
                )
                largest = higher
            out_ref[span, pl.ds(pl.multiple_of(head * DH, DH), DH)] = (mixed / total).astype(jnp.bfloat16)

    def turn(at, carry):
        @pl.when(at < AH)
        def _():
            head = at

            @pl.when(head + ahead < AH)
            def _():
                send_own(head + ahead)

            arrived(0, head, me >= 4)
            begin((upper == 1) & (me >= 4), 1, head, 0, beside)
            begin((odd == 1) & (me >= 4), 3, head, 0, twin)

        @pl.when((at >= 1) & (at < AH + 1))
        def _():
            head = at - 1
            arrived(1, head, me >= 2)
            begin((odd == 1) & (me >= 2), 2, head, 2, twin)
            begin((odd == 0) & (me >= 2), 3, head, 2, twin)

        @pl.when(at >= 2)
        def _():
            head = at - 2
            arrived(2, head, me >= 1)
            arrived(3, head, me >= 3)
            for copy in own_copies(head):
                copy.wait()
            attend(head)

        return carry

    lax.fori_loop(0, AH + 2, turn, 0)

    def finish(head, carry):
        sent(head)
        return carry

    lax.fori_loop(0, AH, finish, 0)


def local(query_rows, key_rows, value_rows, doc_start, n):
    rows = query_rows.shape[0]
    reach = WINDOW // rows + 1
    docs = jnp.broadcast_to(doc_start[:, None], (rows, DH))
    anywhere = pl.BlockSpec(memory_space=pl.ANY)
    inside = pl.BlockSpec(memory_space=pltpu.VMEM)
    return pl.pallas_call(
        functools.partial(kernel, n, rows, AH),
        out_shape=jax.ShapeDtypeStruct(query_rows.shape, jnp.bfloat16),
        in_specs=[inside, anywhere, anywhere, anywhere],
        out_specs=inside,
        scratch_shapes=[
            pltpu.VMEM((AH, rows, DH), jnp.bfloat16),
            pltpu.VMEM((AH, reach * rows, DH), jnp.bfloat16),
            pltpu.VMEM((AH, reach * rows, DH), jnp.bfloat16),
            pltpu.VMEM((rows, DH), jnp.int32),
            pltpu.SemaphoreType.DMA((3, AH)),
            pltpu.SemaphoreType.DMA((4, 2, AH)),
            pltpu.SemaphoreType.DMA((4, 2, AH)),
        ],
        compiler_params=pltpu.CompilerParams(
            collective_id=0, has_side_effects=True, vmem_limit_bytes=48 * 1024 * 1024
        ),
    )(docs, query_rows, key_rows, value_rows)


def solution(mesh):
    placed = (
        P(("grp", "seq"), None),
        P(("grp", "seq"), None),
        P(("grp", "seq"), None),
        P(("grp", "seq")),
    )
    return jax.shard_map(
        functools.partial(local, n=mesh.shape["seq"]),
        mesh=mesh, in_specs=placed, out_specs=P(("grp", "seq"), None), check_vma=False,
    )
```

time: 398 us -> 89.7 us (0.23)
  waiting for transfers between devices: 227 us -> 0 us
  local copies, waits for them, and re-layouts: 98.7 us -> 4.76 us
  Pallas kernels: 0 us -> 84.7 us
  matrix products: 42.8 us -> 0 us
  other arithmetic: 12.6 us -> 0 us
  loops' own time: 8.39 us -> 0 us
  starting transfers between devices: 8 us -> 0 us
    ppermute x4 -> x0, waiting for transfers between devices: 227 us -> none  [shifted(): return lax.ppermute(block, axis, route)]
    pallas_call x0 -> x1, Pallas kernels: none -> 84.7 us  [local(): pl.pallas_call(functools.partial(kernel, n, rows, AH), out_shape=jax.Shap...]
    slice x12 -> x0, local copies, waits for them, and re-layouts: 74.5 us -> none  [one_head(): value_one = lax.dynamic_slice_in_dim(gathered[1], column, DH, 1)]
    dot_general x24 -> x0, matrix products: 42.8 us -> none  [the longest x12 31.6 us: one_head(): jnp.einsum('qd,kd->qk', query_one, key_one, preferred_element_type=jnp.fl...]
    reduce_sum x12 -> x0, other arithmetic: 10.2 us -> none  [one_head(): totals = jnp.sum(powers, axis=1, keepdims=True)]
    unnamed x14 -> x5, local copies, waits for them, and re-layouts: 14 us -> 3.96 us
    another operation x1 -> x0, loops' own time: 8.39 us -> none  [local(): head_outputs = lax.map(one_head, jnp.arange(AH, dtype=jnp.int32))]
    ppermute x4 -> x0, starting transfers between devices: 8 us -> none  [shifted(): return lax.ppermute(block, axis, route)]
  transfers between devices with their start and end apart: 4 -> 0, of which waited for: 4 -> 0; matrix products, arithmetic and copies ran while one was open for 2% -> 0% of each run, Pallas kernels for 0% -> 0%
where the time goes in v1:
time: 89.7 us; the launch traced here: 89.5 us
  Pallas kernels  84.7 us (94%)
  local copies, waits for them, and re-layouts  4.76 us (5%)
    pallas_call x1, Pallas kernels, local(): pl.pallas_call(functools.partial(kernel, n, rows, AH), out_shape=jax.Shap...  84.7 us
    unnamed x5, local copies, waits for them, and re-layouts  3.96 us

profile of v1, /device:TPU:24, one launch (start us, length us, event | category | flops | bytes accessed | tf_op | source)
XLA Modules:
  0.0 89.5 jit_solution(4240573156778844227)
XLA Ops:
  0.0 0.8 broadcast_in_dim.2.doc_ref
  0.8 0.0 copy-start
  0.8 1.4 %copy-done = bf16[512,1536]{1,0:T(8,128)(2,1)S(1)} copy-done((bf16[512,1536]{1,0:T(8,128)(2,1)S(1)}, bf16[512,1536]{1,0:T(8,128)(2,1)}, u32[]{:S(2)}) %copy-start) | copy-done | bytes 1572888
  2.2 0.0 copy-start.1
  2.2 1.4 %copy-done.1 = bf16[512,1536]{1,0:T(8,128)(2,1)S(1)} copy-done((bf16[512,1536]{1,0:T(8,128)(2,1)S(1)}, bf16[512,1536]{1,0:T(8,128)(2,1)}, u32[]{:S(2)}) %copy-start.1) | copy-done | bytes 1572888
  3.6 84.7 %shard_map.46 = bf16[512,1536]{1,0:T(8,128)(2,1)S(1)} custom-call(s32[512,128]{1,0:T(8,128)S(1)} %broadcast_in_dim.2.doc_ref, bf16[512,1536]{1,0:T(8,128)(2,1)S(1)} %copy-done, bf16[512,1536]{1,0:T(8,128)(2,1)S(1)} %copy-done.1, bf16[512,1536]{1,0:T(8,128)(2,1)} %v_hbm.1), custom_call_target="tpu_custom_call" | custom-call | tf_op jit(solution)/shard_map/pallas_call | solution.py:210
  88.3 1.1 %copy.6 = bf16[512,1536]{1,0:T(8,128)(2,1)} copy(bf16[512,1536]{1,0:T(8,128)(2,1)S(1)} %shard_map.46) | data formatting | bytes 3145728
Async XLA Ops:
  0.8 1.4 %copy-start = (bf16[512,1536]{1,0:T(8,128)(2,1)S(1)}, bf16[512,1536]{1,0:T(8,128)(2,1)}, u32[]{:S(2)}) copy-start(bf16[512,1536]{1,0:T(8,128)(2,1)} %q_hbm.1) | copy-start | bytes 4718596
  2.2 1.4 %copy-start.1 = (bf16[512,1536]{1,0:T(8,128)(2,1)S(1)}, bf16[512,1536]{1,0:T(8,128)(2,1)}, u32[]{:S(2)}) copy-start(bf16[512,1536]{1,0:T(8,128)(2,1)} %k_hbm.1) | copy-start | bytes 4718596

commit v2 on v1

v2 whole, which is shorter than its diff:
```python
import functools
import math

import jax
import jax.numpy as jnp
from jax import lax
from jax.experimental import pallas as pl
from jax.experimental.pallas import tpu as pltpu
from jax.sharding import PartitionSpec as P

AH = 12
DH = 128
WINDOW = 2048
MESH = pl.DeviceIdType.MESH
HIDDEN = -1e30


def kernel(n, rows, doc_ref, q_hbm, k_hbm, v_hbm, out_ref,
           q_buf, k_buf, v_buf, low, top_buf, sum_buf, mix_buf, own_sem, send_sem, recv_sem):
    group = lax.axis_index("grp")
    me = lax.axis_index("seq")
    upper = (me // 2) % 2
    odd = me % 2
    beside = me + 2 - 4 * upper
    twin = me + 1 - 2 * odd
    half = rows // 2
    sources = (k_hbm, v_hbm)
    buffers = (k_buf, v_buf)

    def columns(ref, head):
        return ref.at[:, pl.ds(pl.multiple_of(head * DH, DH), DH)]

    def slot(which, head, shard):
        return buffers[which].at[head, pl.ds(shard * rows, rows), :]

    def own_copies(head):
        pairs = [(q_hbm, q_buf.at[head])] + [(sources[w], slot(w, head, 4)) for w in (0, 1)]
        return [
            pltpu.make_async_copy(columns(source, head), target, own_sem.at[at, head])
            for at, (source, target) in enumerate(pairs)
        ]

    landing = (0, 2, 3, 1)

    def copies(kind, head, source_shard, target, which=(0, 1)):
        made = []
        for w in which:
            source = columns(sources[w], head) if source_shard is None else slot(w, head, source_shard)
            made.append(pltpu.make_async_remote_copy(
                src_ref=source,
                dst_ref=slot(w, head, landing[kind]),
                send_sem=send_sem.at[kind, w, head],
                recv_sem=recv_sem.at[kind, w, head],
                device_id=(group, target),
                device_id_type=MESH,
            ))
        return made

    def begin(condition, kind, head, source_shard, target, which=(0, 1)):
        @pl.when(condition)
        def _():
            for copy in copies(kind, head, source_shard, target, which):
                copy.start()

    def arrived(kind, head, condition, which=(0, 1)):
        @pl.when(condition)
        def _():
            for copy in copies(kind, head, None, twin, which):
                copy.wait_recv()

    def send_own(head):
        begin(me + 4 < n, 0, head, None, me + 4)
        begin(upper == 0, 1, head, None, beside)
        begin(odd == 0, 2, head, None, twin)

    def sent(head):
        for kind, condition in (
            (0, me + 4 < n),
            (1, (upper == 0) | (me >= 4)),
            (2, (odd == 0) | (me >= 2)),
            (3, ((odd == 0) & (me >= 2)) | (me >= 5)),
        ):
            @pl.when(condition)
            def _():
                for copy in copies(kind, head, None, twin):
                    copy.wait_send()

    barrier = pltpu.get_barrier_semaphore()
    pl.semaphore_signal(barrier, inc=1, device_id=(group, beside), device_id_type=MESH)
    pl.semaphore_signal(barrier, inc=1, device_id=(group, twin), device_id_type=MESH)

    @pl.when(me >= 4)
    def _():
        pl.semaphore_signal(barrier, inc=1, device_id=(group, me - 4), device_id_type=MESH)

    @pl.when(me + 4 < n)
    def _():
        pl.semaphore_signal(barrier, inc=1, device_id=(group, me + 4), device_id_type=MESH)

    peers = 2 + (me >= 4).astype(jnp.int32) + (me + 4 < n).astype(jnp.int32)
    pl.semaphore_wait(barrier, peers)

    def first(head, carry):
        send_own(head)
        return carry

    lax.fori_loop(0, AH, first, 0)

    def fetch(head, carry):
        for copy in own_copies(head):
            copy.start()
        return carry

    lax.fori_loop(0, AH, fetch, 0)

    for shard in range(4):
        @pl.when(me < 4 - shard)
        def _():
            def clear(head, carry):
                for buffer in buffers:
                    buffer[head, pl.ds(shard * rows, rows), :] = jnp.zeros((rows, DH), jnp.bfloat16)
                return carry

            lax.fori_loop(0, AH, clear, 0)

    row = lax.broadcasted_iota(jnp.int32, (rows, DH), 0)
    starts = jnp.transpose(jnp.broadcast_to(doc_ref[...], (DH, rows)))
    low[...] = jnp.maximum(starts - (me * rows - WINDOW), row + 1)

    scale = math.log2(math.e) / math.sqrt(DH)

    def absorb(state, part, head, spans):
        span = slice(part * half, (part + 1) * half)
        queries = q_buf[head, span, :]
        lowest = low[span, 0:1]
        every = []
        for start, count in spans:
            scores = lax.dot_general(
                queries, k_buf[head, start:start + count, :], (((1,), (1,)), ((), ())),
                preferred_element_type=jnp.float32,
            )
            place = start + lax.broadcasted_iota(jnp.int32, (half, count), 1)
            allowed = place >= lowest
            if start >= WINDOW:
                query = part * half + lax.broadcasted_iota(jnp.int32, (half, count), 0)
                allowed = allowed & (place <= query + WINDOW)
            every.append(jnp.where(allowed, scores, HIDDEN))
        largest = functools.reduce(jnp.maximum, [jnp.max(x, axis=1, keepdims=True) for x in every])
        if state is not None:
            largest = jnp.maximum(largest, state[0])
        total = mixed = 0.0
        if state is not None:
            fade = jnp.exp2((state[0] - largest) * scale)
            total, mixed = state[1] * fade, state[2] * fade
        for (start, count), scores in zip(spans, every):
            powers = jnp.exp2((scores - largest) * scale)
            total = total + jnp.sum(powers, axis=1, keepdims=True)
            mixed = mixed + jnp.dot(
                powers.astype(jnp.bfloat16), v_buf[head, start:start + count, :],
                preferred_element_type=jnp.float32,
            )
        return largest, total, mixed

    def load(head, part):
        span = slice(part * half, (part + 1) * half)
        at = head % 2
        return top_buf[at, span, 0:1], sum_buf[at, span, 0:1], mix_buf[at, span, :]

    def store(head, part, state):
        span = slice(part * half, (part + 1) * half)
        at = head % 2
        top_buf[at, span, 0:1] = state[0]
        sum_buf[at, span, 0:1] = state[1]
        mix_buf[at, span, :] = state[2]

    def turn(at, carry):
        @pl.when(at < AH)
        def _():
            head = at
            for w in (0, 1):
                arrived(0, head, me >= 4, (w,))
                begin((upper == 1) & (me >= 4), 1, head, 0, beside, (w,))
                begin((odd == 1) & (me >= 4), 3, head, 0, twin, (w,))

        @pl.when(at >= 1)
        def _():
            head = at - 1
            for w in (0, 1):
                arrived(1, head, me >= 2, (w,))
                begin((odd == 1) & (me >= 2), 2, head, 2, twin, (w,))
                begin((odd == 0) & (me >= 2), 3, head, 2, twin, (w,))

        @pl.when(at < AH)
        def _():
            head = at
            for copy in own_copies(head):
                copy.wait()
            for part in (0, 1):
                store(head, part, absorb(None, part, head, (
                    (part * half, rows - part * half), (WINDOW, (part + 1) * half)
                )))

        @pl.when(at >= 1)
        def _():
            head = at - 1
            for part in (0, 1):
                store(head, part, absorb(load(head, part), part, head, ((2 * rows, rows),)))
            arrived(2, head, me >= 1)
            arrived(3, head, me >= 3)
            for part in (0, 1):
                span = slice(part * half, (part + 1) * half)
                _, total, mixed = absorb(load(head, part), part, head, ((rows, rows), (3 * rows, rows)))
                out_ref[span, pl.ds(pl.multiple_of(head * DH, DH), DH)] = (mixed / total).astype(jnp.bfloat16)

        return carry

    lax.fori_loop(0, AH + 1, turn, 0)

    def finish(head, carry):
        sent(head)
        return carry

    lax.fori_loop(0, AH, finish, 0)


def local(query_rows, key_rows, value_rows, doc_start, n):
    rows = query_rows.shape[0]
    reach = WINDOW // rows + 1
    anywhere = pl.BlockSpec(memory_space=pl.ANY)
    inside = pl.BlockSpec(memory_space=pltpu.VMEM)
    return pl.pallas_call(
        functools.partial(kernel, n, rows),
        out_shape=jax.ShapeDtypeStruct(query_rows.shape, jnp.bfloat16),
        in_specs=[inside, anywhere, anywhere, anywhere],
        out_specs=inside,
        scratch_shapes=[
            pltpu.VMEM((AH, rows, DH), jnp.bfloat16),
            pltpu.VMEM((AH, reach * rows, DH), jnp.bfloat16),
            pltpu.VMEM((AH, reach * rows, DH), jnp.bfloat16),
            pltpu.VMEM((rows, DH), jnp.int32),
            pltpu.VMEM((2, rows, DH), jnp.float32),
            pltpu.VMEM((2, rows, DH), jnp.float32),
            pltpu.VMEM((2, rows, DH), jnp.float32),
            pltpu.SemaphoreType.DMA((3, AH)),
            pltpu.SemaphoreType.DMA((4, 2, AH)),
            pltpu.SemaphoreType.DMA((4, 2, AH)),
        ],
        compiler_params=pltpu.CompilerParams(
            collective_id=0, has_side_effects=True, vmem_limit_bytes=60 * 1024 * 1024
        ),
    )(doc_start.reshape(1, rows), query_rows, key_rows, value_rows)


def solution(mesh):
    placed = (
        P(("grp", "seq"), None),
        P(("grp", "seq"), None),
        P(("grp", "seq"), None),
        P(("grp", "seq")),
    )
    return jax.shard_map(
        functools.partial(local, n=mesh.shape["seq"]),
        mesh=mesh, in_specs=placed, out_specs=P(("grp", "seq"), None), check_vma=False,
    )
```

time: 89.7 us -> 86 us (0.959)
  local copies, waits for them, and re-layouts: 4.76 us -> 2.65 us
  Pallas kernels: 84.7 us -> 82.7 us
    pallas_call x1, Pallas kernels: 84.7 us -> 82.7 us  [local(): pl.pallas_call(functools.partial(kernel, n, rows), out_shape=jax.ShapeDty...]
    unnamed x5 -> x1, local copies, waits for them, and re-layouts: 3.96 us -> 2.65 us
where the time goes in v2:
time: 86 us; the launch traced here: 85.4 us
  Pallas kernels  82.7 us (96%)
  local copies, waits for them, and re-layouts  2.65 us (3%)
    pallas_call x1, Pallas kernels, local(): pl.pallas_call(functools.partial(kernel, n, rows), out_shape=jax.ShapeDty...  82.7 us
    unnamed x1, local copies, waits for them, and re-layouts  2.65 us

profile of v2, /device:TPU:24, one launch (start us, length us, event | category | flops | bytes accessed | tf_op | source)
XLA Modules:
  0.0 85.4 jit_solution(16030228109891877608)
XLA Ops:
  0.0 82.7 %shard_map.46 = bf16[512,1536]{1,0:T(8,128)(2,1)} custom-call(s32[1,512]{1,0:T(1,128)} %bitcast.1, bf16[512,1536]{1,0:T(8,128)(2,1)} %q_hbm.1, bf16[512,1536]{1,0:T(8,128)(2,1)} %k_hbm.1, bf16[512,1536]{1,0:T(8,128)(2,1)} %v_hbm.1), custom_call_target="tpu_custom_call" | custom-call | tf_op jit(solution)/shard_map/pallas_call | solution.py:231
  82.7 2.7 %copy.6 = bf16[512,1536]{1,0:T(8,128)(2,1)} copy(bf16[512,1536]{1,0:T(8,128)(2,1)} %shard_map.46) | data formatting | bytes 3145728

commit v3 on v2

--- a/solution.py
+++ b/solution.py
@@ -13,6 +13,8 @@
 WINDOW = 2048
 MESH = pl.DeviceIdType.MESH
 HIDDEN = -1e30
+AHEAD = 3
+PIECES = (1, 1, 1, 1)
 
 
 def kernel(n, rows, doc_ref, q_hbm, k_hbm, v_hbm, out_ref,
@@ -27,63 +29,61 @@
     sources = (k_hbm, v_hbm)
     buffers = (k_buf, v_buf)
 
-    def columns(ref, head):
-        return ref.at[:, pl.ds(pl.multiple_of(head * DH, DH), DH)]
-
-    def slot(which, head, shard):
-        return buffers[which].at[head, pl.ds(shard * rows, rows), :]
+    def columns(ref, head, first, count):
+        return ref.at[pl.ds(first, count), pl.ds(pl.multiple_of(head * DH, DH), DH)]
+
+    def slot(which, head, shard, first, count):
+        return buffers[which].at[head, pl.ds(shard * rows + first, count), :]
 
     def own_copies(head):
-        pairs = [(q_hbm, q_buf.at[head])] + [(sources[w], slot(w, head, 4)) for w in (0, 1)]
+        pairs = [(q_hbm, q_buf.at[head])] + [(sources[w], slot(w, head, 4, 0, rows)) for w in (0, 1)]
         return [
-            pltpu.make_async_copy(columns(source, head), target, own_sem.at[at, head])
+            pltpu.make_async_copy(columns(source, head, 0, rows), target, own_sem.at[at, head])
             for at, (source, target) in enumerate(pairs)
         ]
 
     landing = (0, 2, 3, 1)
 
-    def copies(kind, head, source_shard, target, which=(0, 1)):
+    def copies(kind, head, source_shard, target, which=(0, 1), pieces=None):
         made = []
+        count = rows // PIECES[kind]
         for w in which:
-            source = columns(sources[w], head) if source_shard is None else slot(w, head, source_shard)
-            made.append(pltpu.make_async_remote_copy(
-                src_ref=source,
-                dst_ref=slot(w, head, landing[kind]),
-                send_sem=send_sem.at[kind, w, head],
-                recv_sem=recv_sem.at[kind, w, head],
-                device_id=(group, target),
-                device_id_type=MESH,
-            ))
+            for piece in range(PIECES[kind]) if pieces is None else pieces:
+                if source_shard is None:
+                    source = columns(sources[w], head, piece * count, count)
+                else:
+                    source = slot(w, head, source_shard, piece * count, count)
+                made.append(pltpu.make_async_remote_copy(
+                    src_ref=source,
+                    dst_ref=slot(w, head, landing[kind], piece * count, count),
+                    send_sem=send_sem.at[kind, w, piece, head],
+                    recv_sem=recv_sem.at[kind, w, piece, head],
+                    device_id=(group, target),
+                    device_id_type=MESH,
+                ))
         return made
 
-    def begin(condition, kind, head, source_shard, target, which=(0, 1)):
+    def begin(condition, kind, head, source_shard, target, which=(0, 1), pieces=None):
         @pl.when(condition)
         def _():
-            for copy in copies(kind, head, source_shard, target, which):
+            for copy in copies(kind, head, source_shard, target, which, pieces):
                 copy.start()
 
-    def arrived(kind, head, condition, which=(0, 1)):
+    def arrived(kind, head, condition, which=(0, 1), pieces=None):
         @pl.when(condition)
         def _():
-            for copy in copies(kind, head, None, twin, which):
+            for copy in copies(kind, head, None, twin, which, pieces):
                 copy.wait_recv()
+
+    def gone(kind, head, condition):
+        @pl.when(condition)
+        def _():
+            for copy in copies(kind, head, None, twin):
+                copy.wait_send()
 
     def send_own(head):
         begin(me + 4 < n, 0, head, None, me + 4)
         begin(upper == 0, 1, head, None, beside)
-        begin(odd == 0, 2, head, None, twin)
-
-    def sent(head):
-        for kind, condition in (
-            (0, me + 4 < n),
-            (1, (upper == 0) | (me >= 4)),
-            (2, (odd == 0) | (me >= 2)),
-            (3, ((odd == 0) & (me >= 2)) | (me >= 5)),
-        ):
-            @pl.when(condition)
-            def _():
-                for copy in copies(kind, head, None, twin):
-                    copy.wait_send()
 
     barrier = pltpu.get_barrier_semaphore()
     pl.semaphore_signal(barrier, inc=1, device_id=(group, beside), device_id_type=MESH)
@@ -100,8 +100,11 @@
     peers = 2 + (me >= 4).astype(jnp.int32) + (me + 4 < n).astype(jnp.int32)
     pl.semaphore_wait(barrier, peers)
 
+    for head in range(AHEAD):
+        send_own(head)
+
     def first(head, carry):
-        send_own(head)
+        begin(odd == 0, 2, head, None, twin)
         return carry
 
     lax.fori_loop(0, AH, first, 0)
@@ -177,9 +180,17 @@
         @pl.when(at < AH)
         def _():
             head = at
+            gone(0, head, me + 4 < n)
+            gone(1, head, upper == 0)
+
+            @pl.when(head + AHEAD < AH)
+            def _():
+                send_own(head + AHEAD)
+
             for w in (0, 1):
-                arrived(0, head, me >= 4, (w,))
-                begin((upper == 1) & (me >= 4), 1, head, 0, beside, (w,))
+                for piece in range(PIECES[0]):
+                    arrived(0, head, me >= 4, (w,), (piece,))
+                    begin((upper == 1) & (me >= 4), 1, head, 0, beside, (w,), (piece,))
                 begin((odd == 1) & (me >= 4), 3, head, 0, twin, (w,))
 
         @pl.when(at >= 1)
@@ -217,7 +228,9 @@
     lax.fori_loop(0, AH + 1, turn, 0)
 
     def finish(head, carry):
-        sent(head)
+        gone(1, head, (upper == 1) & (me >= 4))
+        gone(2, head, (odd == 0) | (me >= 2))
+        gone(3, head, ((odd == 0) & (me >= 2)) | (me >= 5))
         return carry
 
     lax.fori_loop(0, AH, finish, 0)
@@ -226,7 +239,7 @@
 def local(query_rows, key_rows, value_rows, doc_start, n):
     rows = query_rows.shape[0]
     reach = WINDOW // rows + 1
-    anywhere = pl.BlockSpec(memory_space=pl.ANY)
+    anywhere = pl.BlockSpec(memory_space=pltpu.HBM)
     inside = pl.BlockSpec(memory_space=pltpu.VMEM)
     return pl.pallas_call(
         functools.partial(kernel, n, rows),
@@ -242,11 +255,11 @@
             pltpu.VMEM((2, rows, DH), jnp.float32),
             pltpu.VMEM((2, rows, DH), jnp.float32),
             pltpu.SemaphoreType.DMA((3, AH)),
-            pltpu.SemaphoreType.DMA((4, 2, AH)),
-            pltpu.SemaphoreType.DMA((4, 2, AH)),
+            pltpu.SemaphoreType.DMA((4, 2, max(PIECES), AH)),
+            pltpu.SemaphoreType.DMA((4, 2, max(PIECES), AH)),
         ],
         compiler_params=pltpu.CompilerParams(
-            collective_id=0, has_side_effects=True, vmem_limit_bytes=60 * 1024 * 1024
+            collective_id=0, has_side_effects=True, vmem_limit_bytes=48 * 1024 * 1024
         ),
     )(doc_start.reshape(1, rows), query_rows, key_rows, value_rows)
 

time: 86 us -> 86 us (level)
  Pallas kernels: 82.7 us -> 80.7 us
  local copies, waits for them, and re-layouts: 2.65 us -> 4.64 us
    pallas_call x1, Pallas kernels: 82.7 us -> 80.7 us  [local(): pl.pallas_call(functools.partial(kernel, n, rows), out_shape=jax.ShapeDty...]
    unnamed x1 -> x7, local copies, waits for them, and re-layouts: 2.65 us -> 4.64 us
where the time goes in v3:
time: 86 us; the launch traced here: 85.3 us
  Pallas kernels  80.7 us (94%)
  local copies, waits for them, and re-layouts  4.64 us (5%)
    pallas_call x1, Pallas kernels, local(): pl.pallas_call(functools.partial(kernel, n, rows), out_shape=jax.ShapeDty...  80.7 us
    unnamed x7, local copies, waits for them, and re-layouts  4.64 us

profile of v3, /device:TPU:24, one launch (start us, length us, event | category | flops | bytes accessed | tf_op | source)
XLA Modules:
  0.0 85.3 jit_solution(14381931609555649966)
XLA Ops:
  0.0 0.0 copy-start
  0.0 1.4 %copy-done = bf16[512,1536]{1,0:T(8,128)(2,1)S(1)} copy-done((bf16[512,1536]{1,0:T(8,128)(2,1)S(1)}, bf16[512,1536]{1,0:T(8,128)(2,1)}, u32[]{:S(2)}) %copy-start) | copy-done | bytes 1572888
  1.4 0.0 copy-start.1
  1.4 1.4 %copy-done.1 = bf16[512,1536]{1,0:T(8,128)(2,1)S(1)} copy-done((bf16[512,1536]{1,0:T(8,128)(2,1)S(1)}, bf16[512,1536]{1,0:T(8,128)(2,1)}, u32[]{:S(2)}) %copy-start.1) | copy-done | bytes 1572888
  2.8 0.0 copy-start.2
  2.8 0.7 copy-done.2
  3.5 80.7 %shard_map.46 = bf16[512,1536]{1,0:T(8,128)(2,1)S(1)} custom-call(s32[1,512]{1,0:T(1,128)S(1)} %bitcast.1, bf16[512,1536]{1,0:T(8,128)(2,1)S(1)} %copy-done, bf16[512,1536]{1,0:T(8,128)(2,1)S(1)} %copy-done.1, bf16[512,1536]{1,0:T(8,128)(2,1)} %v_hbm.1), custom_call_target="tpu_custom_call" | custom-call | tf_op jit(solution)/shard_map/pallas_call | solution.py:244
  84.2 1.1 %copy.6 = bf16[512,1536]{1,0:T(8,128)(2,1)} copy(bf16[512,1536]{1,0:T(8,128)(2,1)S(1)} %shard_map.46) | data formatting | bytes 3145728
Async XLA Ops:
  0.0 1.4 %copy-start = (bf16[512,1536]{1,0:T(8,128)(2,1)S(1)}, bf16[512,1536]{1,0:T(8,128)(2,1)}, u32[]{:S(2)}) copy-start(bf16[512,1536]{1,0:T(8,128)(2,1)} %q_hbm.1) | copy-start | bytes 4718596
  1.4 1.4 %copy-start.1 = (bf16[512,1536]{1,0:T(8,128)(2,1)S(1)}, bf16[512,1536]{1,0:T(8,128)(2,1)}, u32[]{:S(2)}) copy-start(bf16[512,1536]{1,0:T(8,128)(2,1)} %k_hbm.1) | copy-start | bytes 4718596
  2.8 0.7 copy-start.2

commit v4 on v3

--- a/solution.py
+++ b/solution.py
@@ -84,6 +84,7 @@
     def send_own(head):
         begin(me + 4 < n, 0, head, None, me + 4)
         begin(upper == 0, 1, head, None, beside)
+        begin(odd == 0, 2, head, None, twin)
 
     barrier = pltpu.get_barrier_semaphore()
     pl.semaphore_signal(barrier, inc=1, device_id=(group, beside), device_id_type=MESH)
@@ -102,12 +103,6 @@
 
     for head in range(AHEAD):
         send_own(head)
-
-    def first(head, carry):
-        begin(odd == 0, 2, head, None, twin)
-        return carry
-
-    lax.fori_loop(0, AH, first, 0)
 
     def fetch(head, carry):
         for copy in own_copies(head):

time: 86 us -> 86 us (level)
  no operation moved by 1% of the time
where the time goes in v4:
time: 86 us; the launch traced here: 85.3 us
  Pallas kernels  80.7 us (94%)
  local copies, waits for them, and re-layouts  4.64 us (5%)
    pallas_call x1, Pallas kernels, local(): pl.pallas_call(functools.partial(kernel, n, rows), out_shape=jax.ShapeDty...  80.7 us
    unnamed x7, local copies, waits for them, and re-layouts  4.64 us

profile of v4, /device:TPU:24, one launch (start us, length us, event | category | flops | bytes accessed | tf_op | source)
XLA Modules:
  0.0 85.3 jit_solution(13384514115396208163)
XLA Ops:
  0.0 0.0 copy-start
  0.0 1.4 %copy-done = bf16[512,1536]{1,0:T(8,128)(2,1)S(1)} copy-done((bf16[512,1536]{1,0:T(8,128)(2,1)S(1)}, bf16[512,1536]{1,0:T(8,128)(2,1)}, u32[]{:S(2)}) %copy-start) | copy-done | bytes 1572888
  1.4 0.0 copy-start.1
  1.4 1.4 %copy-done.1 = bf16[512,1536]{1,0:T(8,128)(2,1)S(1)} copy-done((bf16[512,1536]{1,0:T(8,128)(2,1)S(1)}, bf16[512,1536]{1,0:T(8,128)(2,1)}, u32[]{:S(2)}) %copy-start.1) | copy-done | bytes 1572888
  2.8 0.0 copy-start.2
  2.8 0.7 copy-done.2
  3.5 80.7 %shard_map.46 = bf16[512,1536]{1,0:T(8,128)(2,1)S(1)} custom-call(s32[1,512]{1,0:T(1,128)S(1)} %bitcast.1, bf16[512,1536]{1,0:T(8,128)(2,1)S(1)} %copy-done, bf16[512,1536]{1,0:T(8,128)(2,1)S(1)} %copy-done.1, bf16[512,1536]{1,0:T(8,128)(2,1)} %v_hbm.1), custom_call_target="tpu_custom_call" | custom-call | tf_op jit(solution)/shard_map/pallas_call | solution.py:239
  84.2 1.1 %copy.6 = bf16[512,1536]{1,0:T(8,128)(2,1)} copy(bf16[512,1536]{1,0:T(8,128)(2,1)S(1)} %shard_map.46) | data formatting | bytes 3145728
Async XLA Ops:
  0.0 1.4 %copy-start = (bf16[512,1536]{1,0:T(8,128)(2,1)S(1)}, bf16[512,1536]{1,0:T(8,128)(2,1)}, u32[]{:S(2)}) copy-start(bf16[512,1536]{1,0:T(8,128)(2,1)} %q_hbm.1) | copy-start | bytes 4718596
  1.4 1.4 %copy-start.1 = (bf16[512,1536]{1,0:T(8,128)(2,1)S(1)}, bf16[512,1536]{1,0:T(8,128)(2,1)}, u32[]{:S(2)}) copy-start(bf16[512,1536]{1,0:T(8,128)(2,1)} %k_hbm.1) | copy-start | bytes 4718596
  2.8 0.7 copy-start.2
